TPU v7x, 32 devices: a whole 2x2x4 slice. The times are simulated.
32 devices in a mesh: groups: 2 (over y), row: 16 (over z, x, core).
Axes of the slice: x: 2, y: 2, z: 4, core: 2. Of those that a mesh axis runs over, the one named last changes fastest.
Arguments:
- object_tiles: bfloat16 [8192, 2, 2048], P(('groups', 'row')), parts along dimension 0, may hold values from -4 to 4
- probe: float32 [4, 256, 2, 256], replicated, may hold values from -3 to 3
- measured: bfloat16 [192, 256, 256], P(('groups', 'row')), parts along dimension 0, may hold values from 0.19921875 to 2.5
- offset_row: int32 [192], P(('groups', 'row')), parts along dimension 0, may hold values from 0 to 255
- offset_col: int32 [192], P(('groups', 'row')), parts along dimension 0, may hold values from 0 to 1791
- subpixel: int32 [192], P(('groups', 'row')), parts along dimension 0, may hold values from 0 to 15
- live_count: int32 [32], P(('groups', 'row')), parts along dimension 0, may hold values from 1 to 6, 48 in all
Outputs:
- object_grad: float32 [8192, 2, 2048], P(('groups', 'row')), parts along dimension 0
- probe_grad: float32 [8, 256, 2, 256], P('groups'), parts along dimension 0
- position_grad: float32 [2, 192], P(None, ('groups', 'row')), parts along dimension 1
There are 2 independent parts, one for each index of `groups`. A program takes and returns all parts, laid end to end along the dimension named above; an argument that names none is the same for every part. Nothing has to cross between parts.
Inputs may be any that keep to these rules, and one draw needn't show every extreme that they name: Device d's live slots are its first live_count[d] slots; live_count sums to 48 and reaches 6 on some device.
All inputs are finite; a program needn't handle non-finite values.
Results may differ from a plain program's by a relative error of at most 0.0099.
Values may be sent and summed in bfloat16 or wider, within the bound.
A program may use at most 128 MiB of HBM per device.

v0:
```python
import math
import jax
import jax.numpy as jnp
from jax import lax
from jax.sharding import PartitionSpec as P


def passed_along(x, axis, by):
    length = lax.axis_size(axis)
    pairs = [(i, i + by) for i in range(length) if 0 <= i + by < length]
    return lax.ppermute(x, axis, pairs)


def dft_tables(patch):
    index = jnp.arange(patch, dtype=jnp.int32)
    phase = index[:, None] * index[None, :] % patch
    angle = phase.astype(jnp.float32) * (2.0 * math.pi / patch)
    scale = 1.0 / math.sqrt(patch)
    cosine = (jnp.cos(angle) * scale).astype(jnp.bfloat16)
    sine = (jnp.sin(angle) * scale).astype(jnp.bfloat16)
    along_x = jnp.concatenate(
        [jnp.concatenate([cosine, -sine], 1), jnp.concatenate([sine, cosine], 1)], 0
    )
    along_y = jnp.concatenate(
        [
            jnp.stack([cosine, sine], -1).reshape(patch, 2 * patch),
            jnp.stack([-sine, cosine], -1).reshape(patch, 2 * patch),
        ],
        0,
    )
    inverse_y = jnp.stack(
        [jnp.concatenate([cosine, -sine], 1), jnp.concatenate([sine, cosine], 1)], 1
    ).reshape(2 * patch, 2 * patch)
    inverse_x = jnp.concatenate(
        [jnp.concatenate([cosine, sine], 1), jnp.concatenate([-sine, cosine], 1)], 0
    )
    return (along_x, along_y, inverse_y, inverse_x)


def fractions(code):
    return ((code // 4).astype(jnp.float32) * 0.25, (code % 4).astype(jnp.float32) * 0.25)


def interpolate(window, code):
    frac_y, frac_x = fractions(code)
    cells = window.astype(jnp.float32)
    size = cells.shape[0] - 1
    upper = (1.0 - frac_x) * cells[:size, :, :size] + frac_x * cells[:size, :, 1:]
    lower = (1.0 - frac_x) * cells[1:, :, :size] + frac_x * cells[1:, :, 1:]
    return (1.0 - frac_y) * upper + frac_y * lower


def spread(grad_patch, frac_y, frac_x):

    def sideways(part):
        return jnp.pad((1.0 - frac_x) * part, ((0, 0), (0, 0), (0, 1))) + jnp.pad(
            frac_x * part, ((0, 0), (0, 0), (1, 0))
        )

    upper = sideways((1.0 - frac_y) * grad_patch)
    lower = sideways(frac_y * grad_patch)
    return jnp.pad(upper, ((0, 1), (0, 0), (0, 0))) + jnp.pad(lower, ((1, 0), (0, 0), (0, 0)))


def slopes(window, grad_patch, frac_y, frac_x):
    cells = window.astype(jnp.float32)
    size = cells.shape[0] - 1
    down = cells[1:] - cells[:size]
    slope_y = (1.0 - frac_x) * down[:, :, :size] + frac_x * down[:, :, 1:]
    across = cells[:, :, 1:] - cells[:, :, :size]
    slope_x = (1.0 - frac_y) * across[:size] + frac_y * across[1:]
    return (jnp.sum(grad_patch * slope_y) / size, jnp.sum(grad_patch * slope_x) / size)


def project(patch_obj, amplitude, probe, tables):
    along_x, along_y, inverse_y, inverse_x = tables
    modes = probe.shape[0]
    size = probe.shape[1]
    preal = probe[:, :, 0, :]
    pimag = probe[:, :, 1, :]
    oreal = patch_obj[:, 0, :]
    oimag = patch_obj[:, 1, :]
    wave = jnp.stack([preal * oreal - pimag * oimag, preal * oimag + pimag * oreal], axis=2).astype(
        jnp.bfloat16
    )
    first = jnp.dot(
        wave.reshape(modes * size, 2 * size), along_x, preferred_element_type=jnp.float32
    ).astype(jnp.bfloat16)
    far = jnp.einsum(
        "ab,mbk->mak",
        along_y,
        first.reshape(modes, 2 * size, size),
        preferred_element_type=jnp.float32,
    )
    far = far.reshape(modes, 2, size, size)
    modulus = jnp.maximum(jnp.sqrt(jnp.sum(far * far, axis=(0, 1))), 0.5)
    ratio = 1.0 - amplitude.astype(jnp.float32) / modulus
    error = (far * ratio).astype(jnp.bfloat16)
    back = jnp.einsum(
        "ab,mbk->mak",
        inverse_y,
        error.reshape(modes, 2 * size, size),
        preferred_element_type=jnp.float32,
    ).astype(jnp.bfloat16)
    exit_grad = jnp.dot(
        back.reshape(modes * size, 2 * size), inverse_x, preferred_element_type=jnp.float32
    ).reshape(modes, size, 2, size)
    ureal = exit_grad[:, :, 0, :]
    uimag = exit_grad[:, :, 1, :]
    obj_grad = jnp.stack(
        [jnp.sum(preal * ureal + pimag * uimag, 0), jnp.sum(preal * uimag - pimag * ureal, 0)],
        axis=1,
    )
    probe_term = jnp.stack([oreal * ureal + oimag * uimag, oreal * uimag - oimag * ureal], axis=2)
    return (obj_grad, probe_term)


def shards(object_tiles, probe, measured, offset_row, offset_col, subpixel, live_count):
    rows = object_tiles.shape[0]
    width = object_tiles.shape[2]
    size = probe.shape[1]
    slots = measured.shape[0]
    spare = slots // 2
    tables = dft_tables(size)
    count = live_count[0]
    slot_ids = jnp.arange(slots, dtype=jnp.int32)
    rim = passed_along(object_tiles, "row", -1)
    extended = jnp.concatenate([object_tiles, rim], axis=0)

    def cut(index):
        return lax.dynamic_slice(
            extended, (offset_row[index], 0, offset_col[index]), (size + 1, 2, size + 1)
        )

    windows = lax.map(cut, slot_ids)
    empty_grads = jnp.zeros((slots + spare, size, 2, size), jnp.float32)
    empty_probe = jnp.zeros(probe.shape, jnp.float32)

    def own_slot(index, carry):
        grads, probe_acc = carry
        patch_obj = interpolate(windows[index], subpixel[index])
        obj_grad, probe_term = project(patch_obj, measured[index], probe, tables)
        return (grads.at[index].set(obj_grad), probe_acc + probe_term)

    grads, probe_acc = lax.fori_loop(0, count, own_slot, (empty_grads, empty_probe))
    probe_grad = lax.psum(probe_acc, "row")

    def settle(index, carry):
        grad_ext, moved = carry
        frac_y, frac_x = fractions(subpixel[index])
        obj_grad = grads[index]
        corner = (offset_row[index], 0, offset_col[index])
        region = lax.dynamic_slice(grad_ext, corner, (size + 1, 2, size + 1))
        grad_ext = lax.dynamic_update_slice(
            grad_ext, region + spread(obj_grad, frac_y, frac_x), corner
        )
        slope_y, slope_x = slopes(windows[index], obj_grad, frac_y, frac_x)
        moved = moved.at[:, index].set(jnp.stack([slope_y, slope_x]))
        return (grad_ext, moved)

    start = (jnp.zeros((rows + size, 2, width), jnp.float32), jnp.zeros((2, slots), jnp.float32))
    grad_ext, moved = lax.fori_loop(0, count, settle, start)
    own_rows = grad_ext[:rows]
    below = passed_along(grad_ext[rows:], "row", 1)
    object_grad = own_rows.at[:size].add(below)
    return (object_grad, probe_grad, moved)


def solution(mesh):
    in_specs = (
        P(("groups", "row"), None, None),
        P(),
        P(("groups", "row"), None, None),
        P(("groups", "row")),
        P(("groups", "row")),
        P(("groups", "row")),
        P(("groups", "row")),
    )
    out_specs = (
        P(("groups", "row"), None, None),
        P("groups", None, None, None),
        P(None, ("groups", "row")),
    )
    return jax.shard_map(shards, mesh=mesh, in_specs=in_specs, out_specs=out_specs, check_vma=False)
```

profile of v0, /device:TPU:0, one launch (start us, length us, event | category | flops | bytes accessed | tf_op | source)
XLA Modules:
  0.0 838.3 jit_solution(12319592840080099803)
XLA Ops:
  18.2 9.6 %pad_maximum_fusion.1 = bf16[512,2,2048]{2,1,0:T(2,128)(2,1)} fusion(bf16[256,2,2048]{2,1,0:T(2,128)(2,1)} %collective-permute-done, bf16[256,2,2048]{2,1,0:T(2,128)(2,1)} %param.21), kind=kLoop, calls=%fused_computation.72 | loop fusion | flops 2097152 | bytes 8388608 | tf_op jit(solution)/shard_map/concatenate | solution.py:128
  27.8 56.9 %while.42 = (s32[]{:T(128)}, bf16[6,257,2,257]{3,2,1,0:T(2,128)(2,1)}, s32[6]{0:T(128)S(1)}, s32[6]{0:T(128)S(1)}, s32[6]{0:T(128)S(1)}, /*index=5*/bf16[512,2,2...) while((s32[]{:T(128)}, bf16[6,257,2,257]{3,2,1,0:T(2,128)(2,1)}, ...), condition=%wide.region_1.2_spmd, body=%wide.region_0.1_spmd.sunk | while | flops 11 | bytes 789771 | solution.py:135
  34.6 2.6 bitcast_dynamic-update-slice_fusion.2
  44.1 2.6 bitcast_dynamic-update-slice_fusion.2
  53.5 2.6 bitcast_dynamic-update-slice_fusion.2
  62.9 2.6 bitcast_dynamic-update-slice_fusion.2
  72.2 2.6 bitcast_dynamic-update-slice_fusion.2
  81.7 2.6 bitcast_dynamic-update-slice_fusion.2
  86.2 3.6 broadcast_in_dim.22
  89.9 32.7 %while.43 = (s32[]{:T(128)}, f32[9,256,2,256]{3,2,1,0:T(2,128)}, f32[4,256,2,256]{3,1,2,0:T(8,128)}, s32[]{:T(128)}, f32[4,256,2,256]{3,1,2,0:T(8,128)S(1)}, /*i...) while((s32[]{:T(128)}, f32[9,256,2,256]{3,2,1,0:T(2,128)}, ...), condition=%wide.region_8.9_spmd, body=%wide.region_2.8_spmd.sunk | while | flops 2159608832 | bytes 92680056 | solution.py:145
  102.6 4.0 fusion.77
  114.7 1.8 fusion.80
  118.6 3.1 fusion.81
  122.6 7.5 broadcast_in_dim.21
  130.2 68.5 %while.44 = (s32[]{:T(128)}, f32[512,2,2048]{2,1,0:T(2,128)}, f32[2,6]{0,1:T(8,128)S(1)}, s32[]{:T(128)}, s32[6]{0:T(128)S(1)}, /*index=5*/s32[6]{0:T(128)S(1)},...) while((s32[]{:T(128)}, f32[512,2,2048]{2,1,0:T(2,128)}, ...), condition=%wide.region_13.14_spmd, body=%wide.region_9.13_spmd.sunk | while | flops 3019835 | bytes 15514405 | solution.py:162
  141.8 3.0 fusion.84
  148.3 2.2 add_add_fusion.2
  150.5 47.5 %dynamic_update_slice.14 = f32[512,2,2048]{2,1,0:T(2,128)} dynamic-update-slice(f32[512,2,2048]{2,1,0:T(2,128)} %get-tuple-element.846, f32[257,2,257]{2,1,0:T(2,128)S(1)} %add_add_fusion.2, s32[]{:T(128)S(6)} %select_n.184, s32[]{:T(128)} %constant.305.clone.1..sunk.2, s32[]{:T(128)S(6)} %select_n.185) | dynamic-update-slice | bytes 1056788 | tf_op jit(solution)/shard_map/while/body/dynamic_update_slice | solution.py:154
  198.7 6.3 slice.174
  204.9 321.3 %collective-permute-start.1 = (f32[256,2,2048]{2,1,0:T(2,128)}, f32[256,2,2048]{2,1,0:T(2,128)}, u32[]{:S(2)}, u32[]{:S(2)}) collective-permute-start(f32[256,2,2048]{2,1,0:T(2,128)} %slice.174), channel_id=1, source_target_pairs={{0,1},{1,2},{2,3},{3,4},{4,5},{5,6},{6,7},{7,8},{8,9},{9,10},{10,1... | collective-permute-start | bytes 12582920 | tf_op jit(solution)/shard_map/ppermute | solution.py:11
  526.3 2.9 copy.50
  531.2 9.5 %slice_add_fusion = f32[256,2,2048]{2,1,0:T(2,128)} fusion(f32[256,2,2048]{2,1,0:T(2,128)} %collective-permute-done.1, f32[512,2,2048]{2,1,0:T(2,128)} %get-tuple-element.358), kind=kLoop, calls=%fused_computation.73 | loop fusion | flops 1048576 | bytes 12582912 | tf_op jit(solution)/shard_map/add | solution.py:165
  540.7 287.0 %all-reduce.8.cloned.1.call-done = f32[4,256,2,256]{3,2,1,0:T(2,128)} async-done(((f32[4,256,2,256]{3,2,1,0:T(2,128)}), f32[4,256,2,256]{3,2,1,0:T(2,128)}) %all-reduce.8.cloned.1.call-update) | async-done | bytes 2097168 | tf_op jit(solution)/shard_map/psum | solution.py:146
  827.6 3.6 copy.102
  (110 shorter events, 51.4 us)
Async XLA Ops:
  7.2 820.5 %all-reduce.8.cloned.1.call-start = ((), (), s32[]{:S(2)}) async-start(), calls=%async_computation | async-start | bytes 4194304 | tf_op jit(solution)/shard_map/psum | solution.py:146
  7.2 11.0 %collective-permute-start = (bf16[256,2,2048]{2,1,0:T(2,128)(2,1)}, bf16[256,2,2048]{2,1,0:T(2,128)(2,1)}, u32[]{:S(2)}, u32[]{:S(2)}) collective-permute-start(bf16[256,2,2048]{2,1,0:T(2,128)(2,1)} %param.21), channel_id=1, source_target_pairs={{1,0},{2,1},{3,2},{4,3},{5,4},{6,5},{7,6},{8,7},{9,8},{10,9},{11,1... | collective-permute-start | bytes 6291464 | tf_op jit(solution)/shard_map/ppermute | solution.py:11
  18.1 9.7 %copy-start.11 = (s32[6]{0:T(128)S(1)}, s32[6]{0:T(128)}, u32[]{:S(2)}) copy-start(s32[6]{0:T(128)} %param.24) | copy-start | bytes 76
  18.2 9.7 %copy-start.12 = (s32[6]{0:T(128)S(1)}, s32[6]{0:T(128)}, u32[]{:S(2)}) copy-start(s32[6]{0:T(128)} %param.25) | copy-start | bytes 76
  86.2 3.7 copy-start.10
  86.2 3.7 copy-start.13
  90.5 6.5 copy-start.6
  90.6 8.9 %copy-start.8 = (bf16[512,512]{1,0:T(8,128)(2,1)}, bf16[512,512]{1,0:T(8,128)(2,1)S(1)}, u32[]{:S(2)}) copy-start(bf16[512,512]{1,0:T(8,128)(2,1)S(1)} %get-tuple-element.804) | copy-start | bytes 1572868 | tf_op jit(solution)/shard_map/while
  97.4 0.7 copy-start.4
  108.5 1.6 copy-start
  114.7 1.8 copy-start.5
  116.5 1.6 copy-start.1
  118.1 3.7 copy-start.7
  118.1 3.7 copy-start.9
  118.6 3.2 copy-start.2
  198.7 327.6 %copy-start.3 = (f32[4,256,2,256]{3,1,2,0:T(8,128)S(1)}, f32[4,256,2,256]{3,1,2,0:T(8,128)}, u32[]{:S(2)}) copy-start(f32[4,256,2,256]{3,1,2,0:T(8,128)} %get-tuple-element.359) | copy-start | bytes 6291460
  204.9 326.3 %collective-permute-start.1 = (f32[256,2,2048]{2,1,0:T(2,128)}, f32[256,2,2048]{2,1,0:T(2,128)}, u32[]{:S(2)}, u32[]{:S(2)}) collective-permute-start(f32[256,2,2048]{2,1,0:T(2,128)} %slice.174), channel_id=1, source_target_pairs={{0,1},{1,2},{2,3},{3,4},{4,5},{5,6},{6,7},{7,8},{8,9},{9,10},{10,1... | collective-permute-start | bytes 12582920 | tf_op jit(solution)/shard_map/ppermute | solution.py:11
Sparse Core Ops, SparseCore 0:
  529.4 298.2 all-reduce.7
where the time goes:
time: 853 us; the launch traced here: 838 us
  starting transfers between devices  323 us (38%)
  waiting for transfers between devices  288 us (34%)
  local copies, waits for them, and re-layouts  119 us (14%)
  loops' own time  43.8 us (5%)
  other arithmetic  40.6 us (5%)
  between operations  14.5 us (2%)
  matrix products  9.26 us (1%)
    ppermute x2, starting transfers between devices, passed_along(): return lax.ppermute(x, axis, pairs)  323 us
    psum x1, waiting for transfers between devices, shards(): probe_grad = lax.psum(probe_acc, 'row')  287 us
    dynamic_update_slice x1, local copies, waits for them, and re-layouts, settle(): lax.dynamic_update_slice(grad_ext, region + spread(obj_grad, frac_y, frac...  47.5 us
    another operation x1, loops' own time, shards(): windows = lax.map(cut, slot_ids)  30.8 us
  transfers between devices with their start and end apart: 3, of which 2 were waited for; matrix products, arithmetic and copies ran while one was open for 3% of the time, Pallas kernels for 0%

commit v1 on v0

--- a/solution.py
+++ b/solution.py
@@ -143,7 +143,7 @@
         return (grads.at[index].set(obj_grad), probe_acc + probe_term)
 
     grads, probe_acc = lax.fori_loop(0, count, own_slot, (empty_grads, empty_probe))
-    probe_grad = lax.psum(probe_acc, "row")
+    probe_grad = jnp.sum(jax.lax.all_gather(probe_acc, axis_name="row"), axis=0)
 
     def settle(index, carry):
         grad_ext, moved = carry

time: 853 us -> 837 us (0.981)
  the two profiles are of different devices: /device:TPU:0 before, /device:TPU:24 now
where the time goes in v1:
time: 837 us; the launch traced here: 822 us
  waiting for transfers between devices  469 us (56%)
  local copies, waits for them, and re-layouts  118 us (14%)
  starting transfers between devices  109 us (13%)
  other arithmetic  53.4 us (6%)
  loops' own time  48.3 us (6%)
  between operations  14.4 us (2%)
  matrix products  10.3 us (1%)
    ppermute x2, waiting for transfers between devices, passed_along(): return lax.ppermute(x, axis, pairs)  469 us
    ppermute x2, starting transfers between devices, passed_along(): return lax.ppermute(x, axis, pairs)  108 us
    dynamic_update_slice x1, local copies, waits for them, and re-layouts, settle(): lax.dynamic_update_slice(grad_ext, region + spread(obj_grad, frac_y, frac...  47.5 us
    another operation x1, loops' own time, shards(): windows = lax.map(cut, slot_ids)  35.4 us
  transfers between devices with their start and end apart: 3, of which 2 were waited for; matrix products, arithmetic and copies ran while one was open for 12% of the time, Pallas kernels for 0%

profile of v1, /device:TPU:24, one launch (start us, length us, event | category | flops | bytes accessed | tf_op | source)
XLA Modules:
  0.0 821.6 jit_solution(7800901032170313695)
XLA Ops:
  7.2 2.7 collective-permute-start
  21.2 12.6 %collective-permute-done = bf16[256,2,2048]{2,1,0:T(2,128)(2,1)} collective-permute-done((bf16[256,2,2048]{2,1,0:T(2,128)(2,1)}, bf16[256,2,2048]{2,1,0:T(2,128)(2,1)}, u32[]{:S(2)}, u32[]{:S(2)}) %collective-permute-start) | collective-permute-done | bytes 2097184 | tf_op jit(solution)/shard_map/ppermute | solution.py:11
  33.8 9.6 %pad_maximum_fusion.1 = bf16[512,2,2048]{2,1,0:T(2,128)(2,1)} fusion(bf16[256,2,2048]{2,1,0:T(2,128)(2,1)} %collective-permute-done, bf16[256,2,2048]{2,1,0:T(2,128)(2,1)} %param.21), kind=kLoop, calls=%fused_computation.72 | loop fusion | flops 2097152 | bytes 8388608 | tf_op jit(solution)/shard_map/concatenate | solution.py:128
  43.4 61.7 %while.42 = (s32[]{:T(128)}, bf16[6,257,2,257]{3,2,1,0:T(2,128)(2,1)}, s32[6]{0:T(128)S(1)}, s32[6]{0:T(128)S(1)}, s32[6]{0:T(128)S(1)}, /*index=5*/bf16[512,2,2...) while((s32[]{:T(128)}, bf16[6,257,2,257]{3,2,1,0:T(2,128)(2,1)}, ...), condition=%wide.region_1.2_spmd, body=%wide.region_0.1_spmd.sunk | while | flops 11 | bytes 790271 | solution.py:135
  51.0 2.6 bitcast_dynamic-update-slice_fusion.2
  71.4 2.6 bitcast_dynamic-update-slice_fusion.2
  81.6 2.6 bitcast_dynamic-update-slice_fusion.2
  91.9 2.7 bitcast_dynamic-update-slice_fusion.2
  102.1 2.6 bitcast_dynamic-update-slice_fusion.2
  105.2 3.6 broadcast_in_dim.22
  110.3 35.1 %while.43 = (s32[]{:T(128)}, f32[9,256,2,256]{3,2,1,0:T(2,128)}, f32[4,256,2,256]{3,1,2,0:T(8,128)}, s32[]{:T(128)}, f32[4,256,2,256]{3,1,2,0:T(8,128)S(1)}, /*i...) while((s32[]{:T(128)}, f32[9,256,2,256]{3,2,1,0:T(2,128)}, ...), condition=%wide.region_8.9_spmd, body=%wide.region_2.8_spmd.sunk | while | flops 2159608832 | bytes 84291320 | solution.py:145
  117.9 2.7 convolution_convert_fusion.3
  122.1 3.9 fusion.77
  141.5 3.1 fusion.81
  145.5 7.5 broadcast_in_dim.21
  152.9 68.5 %while.44 = (s32[]{:T(128)}, f32[512,2,2048]{2,1,0:T(2,128)}, f32[2,6]{0,1:T(8,128)S(1)}, s32[]{:T(128)}, s32[6]{0:T(128)S(1)}, /*index=5*/s32[6]{0:T(128)S(1)},...) while((s32[]{:T(128)}, f32[512,2,2048]{2,1,0:T(2,128)}, ...), condition=%wide.region_13.14_spmd, body=%wide.region_9.13_spmd.sunk | while | flops 3019835 | bytes 15514397 | solution.py:162
  158.9 3.1 fusion.84
  170.6 47.5 %dynamic_update_slice.14 = f32[512,2,2048]{2,1,0:T(2,128)} dynamic-update-slice(f32[512,2,2048]{2,1,0:T(2,128)} %get-tuple-element.846, f32[257,2,257]{2,1,0:T(2,128)S(1)} %add_add_fusion.2, s32[]{:T(128)S(6)} %select_n.184, s32[]{:T(128)} %constant.306.clone.1..sunk.2, s32[]{:T(128)S(6)} %select_n.185) | dynamic-update-slice | bytes 1056788 | tf_op jit(solution)/shard_map/while/body/dynamic_update_slice | solution.py:154
  221.5 6.1 slice.174
  227.6 105.8 %collective-permute-start.1 = (f32[256,2,2048]{2,1,0:T(2,128)}, f32[256,2,2048]{2,1,0:T(2,128)}, u32[]{:S(2)}, u32[]{:S(2)}) collective-permute-start(f32[256,2,2048]{2,1,0:T(2,128)} %slice.174), channel_id=1, source_target_pairs={{0,1},{1,2},{2,3},{3,4},{4,5},{5,6},{6,7},{7,8},{8,9},{9,10},{10,1... | collective-permute-start | bytes 12582920 | tf_op jit(solution)/shard_map/ppermute | solution.py:11
  334.0 456.0 %collective-permute-done.1 = f32[256,2,2048]{2,1,0:T(2,128)} collective-permute-done((f32[256,2,2048]{2,1,0:T(2,128)}, f32[256,2,2048]{2,1,0:T(2,128)}, u32[]{:S(2)}, u32[]{:S(2)}) %collective-permute-start.1) | collective-permute-done | bytes 4194336 | tf_op jit(solution)/shard_map/ppermute | solution.py:11
  790.0 9.5 %slice_add_fusion = f32[256,2,2048]{2,1,0:T(2,128)} fusion(f32[256,2,2048]{2,1,0:T(2,128)} %collective-permute-done.1, f32[512,2,2048]{2,1,0:T(2,128)} %get-tuple-element.358), kind=kLoop, calls=%fused_computation.73 | loop fusion | flops 1048576 | bytes 12582912 | tf_op jit(solution)/shard_map/add | solution.py:165
  799.5 12.1 %reduce_sum.76 = f32[4,256,2,256]{3,1,2,0:T(8,128)S(1)} reduce(f32[16,4,256,2,256]{4,2,3,1,0:T(8,128)} %bitcast.178, f32[]{:T(128)} %constant.307.clone.1), dimensions={0}, to_apply=%region_14.15 | reduce | flops 7864320 | bytes 35651588 | tf_op jit(solution)/shard_map/reduce_sum | solution.py:146
  811.6 2.9 copy.48
  (100 shorter events, 56.9 us)
Async XLA Ops:
  7.2 792.3 %all-gather.3.cloned.1.call-start = ((), (), s32[]{:S(2)}) async-start(), calls=%async_computation | async-start | bytes 35651584 | tf_op jit(solution)/shard_map/all_gather | solution.py:146
  7.2 26.6 %collective-permute-start = (bf16[256,2,2048]{2,1,0:T(2,128)(2,1)}, bf16[256,2,2048]{2,1,0:T(2,128)(2,1)}, u32[]{:S(2)}, u32[]{:S(2)}) collective-permute-start(bf16[256,2,2048]{2,1,0:T(2,128)(2,1)} %param.21), channel_id=1, source_target_pairs={{1,0},{2,1},{3,2},{4,3},{5,4},{6,5},{7,6},{8,7},{9,8},{10,9},{11,1... | collective-permute-start | bytes 6291464 | tf_op jit(solution)/shard_map/ppermute | solution.py:11
  21.1 22.3 %copy-start.6 = (s32[6]{0:T(128)S(1)}, s32[6]{0:T(128)}, u32[]{:S(2)}) copy-start(s32[6]{0:T(128)} %param.24) | copy-start | bytes 76
  21.2 22.3 %copy-start.7 = (s32[6]{0:T(128)S(1)}, s32[6]{0:T(128)}, u32[]{:S(2)}) copy-start(s32[6]{0:T(128)} %param.25) | copy-start | bytes 76
  105.2 5.1 copy-start.5
  105.2 5.1 copy-start.8
  115.9 0.7 copy-start.3
  129.0 1.6 copy-start
  135.2 1.8 copy-start.4
  137.0 1.6 copy-start.1
  139.1 1.3 copy-start.2
  227.6 562.4 %collective-permute-start.1 = (f32[256,2,2048]{2,1,0:T(2,128)}, f32[256,2,2048]{2,1,0:T(2,128)}, u32[]{:S(2)}, u32[]{:S(2)}) collective-permute-start(f32[256,2,2048]{2,1,0:T(2,128)} %slice.174), channel_id=1, source_target_pairs={{0,1},{1,2},{2,3},{3,4},{4,5},{5,6},{6,7},{7,8},{8,9},{9,10},{10,1... | collective-permute-start | bytes 12582920 | tf_op jit(solution)/shard_map/ppermute | solution.py:11
Sparse Core Ops, SparseCore 0:
  145.6 380.8 all-gather.2
